TPU v7x, 128 devices: a whole 4x4x4 slice. The times are simulated.
128 devices in a mesh: ang: 8 (over x, core), det: 16 (over z, y).
Axes of the slice: x: 4, y: 4, z: 4, core: 2. Of those that a mesh axis runs over, the one named last changes fastest.
Arguments:
- raw_counts: float32 [256, 128, 4096], P('ang', None, 'det'), may hold values from 0.15 to 0.9
- dark_field: float32 [128, 4096], P(None, 'det'), may hold values from 0 to 0.1
- flat_field: float32 [128, 4096], P(None, 'det'), may hold values from 0.8 to 1.2
- destinations: int32 [32, 1], replicated, may hold values from 0 to 15; in each aligned block of 32 rows (0 to 31, 32 to 63, ...) at most 4 rows name the same one
- band_offsets: int32 [4096], replicated, may hold values from 0 to 4092, as said below
- band_weights: float32 [4, 4096], replicated, may hold values from 0.05 to 0.5
Outputs:
- parallel_slabs: float32 [256, 64, 4, 4096], P('ang', 'det')
Inputs may be any that keep to these rules, and one draw needn't show every extreme that they name: `destinations`: no z-slab owner receives more than 4 row blocks, and some owner receives exactly 4. band_offsets[t] lies between t - 8 and t + 5.
All inputs are finite; a program needn't handle non-finite values.
Results may differ from a plain program's by a relative error of at most 0.0001.
Values sent between devices are 32-bit elements; how exact they have to be, the bound alone decides.
A program may use at most 64 MiB of HBM per device.

v0:
```python
import jax
import jax.numpy as jnp
from jax import lax
from jax.sharding import PartitionSpec as P

RB = 4
SMW = 4
ITERS = 3
HB = 8
BW = 4
MOST = 4
cauchy_scale = 0.2


def with_halo(x, sides, width):
    for axis, dim in sides:
        count, length = (lax.axis_size(axis), x.shape[dim])
        up = [(i, (i + 1) % count) for i in range(count - 1)]
        down = [(j, i) for i, j in up]
        last = lax.slice_in_dim(x, length - width, length, axis=dim)
        leading = lax.slice_in_dim(x, 0, width, axis=dim)
        before = lax.ppermute(last, axis, up)
        after = lax.ppermute(leading, axis, down)
        x = jnp.concatenate([before, x, after], axis=dim)
    return x


def smooth_local(values, first_col, total_cols):
    col_width = values.shape[2]
    padded = with_halo(values, (("det", 2),), SMW)
    summed = padded[:, :, 0:col_width]
    for position in range(1, 2 * SMW + 1):
        summed = summed + padded[:, :, position : position + col_width]
    columns = first_col + jnp.arange(col_width, dtype=jnp.int32)
    counts = jnp.minimum(columns + SMW, total_cols - 1) - jnp.maximum(columns - SMW, 0) + 1
    return summed / counts.astype(jnp.float32)


def band_sum(widened, relative, weights, col_width):
    summed = None
    for shift in range(-HB, HB + 1):
        coeff = jnp.zeros((col_width,), jnp.float32)
        for position in range(BW):
            coeff = coeff + jnp.where(relative == shift - position, weights[position], 0.0)
        term = coeff * widened[..., HB + shift : HB + shift + col_width]
        summed = term if summed is None else summed + term
    return summed


def slot_tables(destinations, owners, most):
    targets = destinations[:, 0]
    block_ids = jnp.arange(targets.shape[0], dtype=jnp.int32)
    same_earlier = (targets[:, None] == targets[None, :]) & (
        block_ids[None, :] < block_ids[:, None]
    )
    slot_rank = jnp.sum(same_earlier.astype(jnp.int32), axis=1)
    owner_ids = jnp.arange(owners, dtype=jnp.int32)
    rank_ids = jnp.arange(most, dtype=jnp.int32)
    matching = (
        (targets[None, None, :] == owner_ids[:, None, None])
        & (slot_rank[None, None, :] == rank_ids[None, :, None])
    ).astype(jnp.int32)
    chosen = jnp.sum(matching * block_ids[None, None, :], axis=2)
    filled = jnp.sum(matching, axis=2)
    return (chosen, filled)


def slot_blocks(values, destinations, owners):
    ang_dev, row_count, col_width = values.shape
    blocks = values.reshape(ang_dev, row_count // RB, RB, col_width)
    chosen, filled = slot_tables(destinations, owners, MOST)
    picked = jnp.take(blocks, chosen.reshape(-1), axis=1).reshape(
        ang_dev, owners, MOST, RB, col_width
    )
    return picked * filled[None, :, :, None, None].astype(jnp.float32)


def body(raw_counts, dark_field, flat_field, destinations, band_offsets, band_weights):
    ang_dev, row_count, col_width = raw_counts.shape
    owners = lax.axis_size("det")
    first_col = lax.axis_index("det") * col_width
    total_cols = col_width * owners
    angles = ang_dev * lax.axis_size("ang")
    projected = -jnp.log((raw_counts - dark_field) / (flat_field - dark_field))
    detail = projected - smooth_local(projected, first_col, total_cols)
    gain_map = lax.psum(jnp.sum(detail, axis=0), "ang") / angles
    for reweight_pass in range(ITERS):
        scaled = (detail - gain_map) / cauchy_scale
        weights = 1.0 / (1.0 + scaled * scaled)
        weighted = jnp.sum(weights * detail, axis=0)
        weight_total = jnp.sum(weights, axis=0)
        total_all, weighted_all = lax.psum((weight_total, weighted), "ang")
        gain_map = weighted_all / total_all
    corrected = projected - gain_map
    picked = slot_blocks(corrected, destinations, owners)
    relative_all = band_offsets - jnp.arange(total_cols, dtype=jnp.int32)
    arrived = lax.all_to_all(picked, "det", split_axis=1, concat_axis=4, tiled=True)
    pad_widths = [(0, 0)] * (arrived.ndim - 1) + [(HB, HB)]
    widened_all = jnp.pad(arrived, pad_widths)
    moved = band_sum(widened_all, relative_all, band_weights, arrived.shape[-1])
    return moved.reshape(ang_dev, MOST, RB, total_cols)


def solution(mesh):
    placed = (P("ang", None, "det"), P(None, "det"), P(None, "det"), P(), P(), P())
    return jax.shard_map(
        body, mesh=mesh, in_specs=placed, out_specs=P("ang", "det", None, None), check_vma=False
    )
```

profile of v0, /device:TPU:6, one launch (start us, length us, event | category | flops | bytes accessed | tf_op | source)
XLA Modules:
  0.0 526.5 jit_solution(13446992526522736455)
XLA Ops:
  6.5 0.0 copy-start.1
  6.5 0.0 copy-start.2
  6.5 0.0 all-reduce.9.cloned.1.call-start
  6.5 5.5 %copy.19 = f32[32,128,256]{1,0,2:T(8,128)} copy(f32[32,128,256]{2,1,0:T(8,128)} %param.6) | data formatting | bytes 8388608 | tf_op args[0]
  12.0 0.0 copy-done.1
  12.0 0.1 copy.18
  12.1 0.0 copy-done.2
  12.2 0.1 copy.20
  12.2 0.0 copy-start.5
  12.3 3.0 log_negate_fusion
  15.3 0.0 copy-start
  15.3 2.0 copy-done
  17.3 3.5 collective-permute-start
  20.8 1.3 collective-permute-start.1
  22.1 0.0 copy-done.5
  22.1 0.5 collective-permute-done
  22.6 4.3 collective-permute-done.1
  26.9 19.3 %fusion.36 = (f32[128,256]{0,1:T(8,128)}, f32[32,128,256]{1,0,2:T(8,128)}) fusion(f32[32,128,256]{1,0,2:T(8,128)} %copy-done, f32[256]{0:T(256)S(1)} %add_convert_fusion, f32[32,128,4]{1,0,2:T(8,128)S(1)} %collective-permute-done.1, f32[32,128,4]{1,0,2:T(8,128)S(1)} %collective-permute-done), kind=kLoop, calls=%fused_computation.112 | loop fusion | flops 19890176 | bytes 8651776 | tf_op jit(solution)/shard_map/reduce_sum | solution.py:86
  46.2 0.0 all-reduce.9.cloned.1.call-update
  46.2 0.0 all-reduce.15.cloned.1.call-start
  46.3 0.2 convert_reduce_fusion
  46.5 61.3 %all-reduce.9.cloned.1.call-done = f32[128,256]{0,1:T(8,128)} async-done(((f32[128,256]{0,1:T(8,128)}), f32[128,256]{0,1:T(8,128)}) %all-reduce.9.cloned.1.call-update) | async-done | bytes 131088 | tf_op jit(solution)/shard_map/psum | solution.py:86
  107.8 0.9 broadcast_multiply_fusion
  108.7 4.8 fusion.29
  113.5 0.0 all-reduce.15.cloned.1.call-update
  113.5 0.0 all-reduce.13.cloned.1.call-start
  113.6 0.2 fusion.33
  113.8 0.1 copy.22
  113.9 0.1 reshape.181
  114.0 59.1 %all-reduce.15.cloned.1.call-done = (f32[128,256]{0,1:T(8,128)}, f32[128,256]{0,1:T(8,128)}) async-done(((f32[128,256]{0,1:T(8,128)}, f32[128,256]{0,1:T(8,128)}), (f32[128,256]{0,1:T(8,128)}, f32[128,256]{0,1:T(8,128)})) %all-reduce.15.cloned.1.call-update) | async-done | bytes 262160 | tf_op jit(solution)/shard_map/psum | solution.py:92
  173.1 1.0 div.57
  174.1 4.8 fusion.30
  178.9 0.0 all-reduce.13.cloned.1.call-update
  179.0 0.2 all-reduce.11.cloned.1.call-start
  179.2 59.4 %all-reduce.13.cloned.1.call-done = (f32[128,256]{0,1:T(8,128)}, f32[128,256]{0,1:T(8,128)}) async-done(((f32[128,256]{0,1:T(8,128)}, f32[128,256]{0,1:T(8,128)}), (f32[128,256]{0,1:T(8,128)}, f32[128,256]{0,1:T(8,128)})) %all-reduce.13.cloned.1.call-update) | async-done | bytes 262160 | tf_op jit(solution)/shard_map/psum | solution.py:92
  238.6 1.0 div.60
  239.6 4.8 fusion.31
  244.4 0.0 all-reduce.11.cloned.1.call-update
  244.4 0.1 copy.17
  244.5 0.1 copy.23
  244.6 59.5 %all-reduce.11.cloned.1.call-done = (f32[128,256]{0,1:T(8,128)}, f32[128,256]{0,1:T(8,128)}) async-done(((f32[128,256]{0,1:T(8,128)}, f32[128,256]{0,1:T(8,128)}), (f32[128,256]{0,1:T(8,128)}, f32[128,256]{0,1:T(8,128)})) %all-reduce.11.cloned.1.call-update) | async-done | bytes 262160 | tf_op jit(solution)/shard_map/psum | solution.py:92
  304.1 1.0 div.63
  305.1 5.4 %broadcast_subtract_fusion = f32[32,128,256]{1,0,2:T(8,128)} fusion(f32[128,256]{0,1:T(8,128)S(1)} %div.63, f32[128,256]{0,1:T(8,128)S(1)} %copy.20, f32[32,128,256]{1,0,2:T(8,128)} %copy.19, f32[128,256]{0,1:T(8,128)S(1)} %copy.18), kind=kLoop, calls=%fused_computation.59 | loop fusion | flops 4194304 | bytes 8781824 | tf_op jit(solution)/shard_map/sub | solution.py:94
  310.5 5.6 %copy.21 = f32[32,128,256]{2,0,1:T(8,128)} copy(f32[32,128,256]{1,0,2:T(8,128)} %broadcast_subtract_fusion) | data formatting | bytes 8388608 | tf_op jit(solution)/shard_map/sub | solution.py:94
  316.1 6.7 %gather_fusion = f32[64,32,4,256]{3,1,2,0:T(8,128)} fusion(f32[32,32,4,256]{3,0,2,1:T(8,128)} %bitcast.18, s32[1024]{0:T(1024)S(1)} %pad_clamp_fusion), kind=kCustom, calls=%fused_computation | custom fusion | bytes 16777472 | tf_op jit(solution)/shard_map/jit(_take)/gather | solution.py:72
  322.8 8.9 %select_multiply_fusion = f32[32,16,4,4,256]{4,0,3,2,1:T(8,128)} fusion(f32[32,16,4,4,256]{4,0,3,2,1:T(8,128)} %bitcast.20, f32[16,4]{1,0:T(8,128)S(1)} %copy.23, pred[16,4]{1,0:T(8,128)(4,1)S(1)} %copy.17), kind=kLoop, calls=%fused_computation.22 | loop fusion | flops 4194304 | bytes 16777536 | tf_op jit(solution)/shard_map/mul | solution.py:75
  331.6 0.0 copy-start.3
  331.6 0.0 copy-start.4
  331.6 7.2 %all-to-all-start = ((f32[32,16,4,4,256]{4,0,3,2,1:T(8,128)}), f32[32,16,4,4,256]{4,0,3,2,1:T(8,128)}, u32[]{:S(2)}, u32[]{:S(2)}) async-start(f32[32,16,4,4,256]{4,0,3,2,1:T(8,128)} %select_multiply_fusion), calls=%async_computation | async-start | bytes 16777216 | tf_op jit(solution)/shard_map/all_to_all | solution.py:97
  338.8 0.0 copy-done.3
  338.9 0.0 copy-done.4
  338.9 0.1 select_add_fusion.16
  339.0 127.9 %all-to-all-done = f32[32,16,4,4,256]{4,0,3,2,1:T(8,128)} async-done(((f32[32,16,4,4,256]{4,0,3,2,1:T(8,128)}), f32[32,16,4,4,256]{4,0,3,2,1:T(8,128)}, u32[]{:S(2)}, u32[]{:S(2)}) %all-to-all-start) | async-done | bytes 8388640 | tf_op jit(solution)/shard_map/all_to_all | solution.py:97
  466.8 4.6 copy.26
  471.5 36.4 %add_bitcast_fusion = f32[32,4,4,4096]{3,0,2,1:T(8,128)} fusion(f32[32,1,4,4,4096]{4,0,3,2,1:T(8,128)S(1)} %bitcast.19, f32[4096]{0:T(1024)S(1)} %get-tuple-element.24, f32[4096]{0:T(1024)S(1)} %get-tuple-element.25, f32[4096]{0:T(1024)S(1)} %get-tuple-element.26, f32[4096]{0:T(1024)S(1)} %get-tuple-element.27, f32[4096]{0:T(1024)S(1)} %get-tuple-element.28, ...), kind=kLoop, calls=%fused_computation.1 | loop fusion | flops 69206016 | bytes 17055744 | tf_op jit(solution)/shard_map/reshape | solution.py:101
  507.8 12.2 %copy.25 = f32[32,4,4,4096]{3,2,1,0:T(4,128)} copy(f32[32,4,4,4096]{3,0,2,1:T(8,128)} %add_bitcast_fusion) | data formatting | bytes 16777216 | tf_op jit(solution)/shard_map/reshape | solution.py:101
  (10 shorter events, 0.1 us)
Async XLA Ops:
  6.5 5.5 %copy-start.1 = (f32[128,256]{1,0:T(8,128)S(1)}, f32[128,256]{1,0:T(8,128)}, u32[]{:S(2)}) copy-start(f32[128,256]{1,0:T(8,128)} %param.7) | copy-start | bytes 393220
  6.5 5.6 %copy-start.2 = (f32[128,256]{1,0:T(8,128)S(1)}, f32[128,256]{1,0:T(8,128)}, u32[]{:S(2)}) copy-start(f32[128,256]{1,0:T(8,128)} %param.8) | copy-start | bytes 393220
  6.5 101.3 %all-reduce.9.cloned.1.call-start = ((), (), s32[]{:S(2)}) async-start(), calls=%async_computation.1 | async-start | bytes 262144 | tf_op jit(solution)/shard_map/psum | solution.py:86
  12.2 9.8 %copy-start.5 = (s32[32,1]{0,1:T(1,128)S(1)}, s32[32,1]{0,1:T(1,128)}, u32[]{:S(2)}) copy-start(s32[32,1]{0,1:T(1,128)} %param.9) | copy-start | bytes 388
  15.3 2.0 copy-start
  17.3 5.4 %collective-permute-start = (f32[32,128,4]{1,0,2:T(8,128)S(1)}, f32[32,128,4]{1,0,2:T(8,128)S(1)}, u32[]{:S(2)}, u32[]{:S(2)}) collective-permute-start(f32[32,128,4]{1,0,2:T(8,128)S(1)} %get-tuple-element.21), channel_id=1, source_target_pairs={{0,1},{1,2},{2,3},{3,4},{4,5},{5,6},{6,7},{7,8},{8,9},{9,10},{10,1... | collective-permute-start | bytes 196616 | tf_op jit(solution)/shard_map/ppermute | solution.py:22
  20.8 6.2 %collective-permute-start.1 = (f32[32,128,4]{1,0,2:T(8,128)S(1)}, f32[32,128,4]{1,0,2:T(8,128)S(1)}, u32[]{:S(2)}, u32[]{:S(2)}) collective-permute-start(f32[32,128,4]{1,0,2:T(8,128)S(1)} %get-tuple-element.22), channel_id=1, source_target_pairs={{1,0},{2,1},{3,2},{4,3},{5,4},{6,5},{7,6},{8,7},{9,8},{10,9},{11,1... | collective-permute-start | bytes 196616 | tf_op jit(solution)/shard_map/ppermute | solution.py:23
  46.2 126.9 %all-reduce.15.cloned.1.call-start = ((), (), s32[]{:S(2)}) async-start(), calls=%async_computation.4 | async-start | bytes 524288 | tf_op jit(solution)/shard_map/psum | solution.py:92
  113.5 125.0 %all-reduce.13.cloned.1.call-start = ((), (), s32[]{:S(2)}) async-start(), calls=%async_computation.3 | async-start | bytes 524288 | tf_op jit(solution)/shard_map/psum | solution.py:92
  179.0 125.1 %all-reduce.11.cloned.1.call-start = ((), (), s32[]{:S(2)}) async-start(), calls=%async_computation.2 | async-start | bytes 524288 | tf_op jit(solution)/shard_map/psum | solution.py:92
  331.6 7.2 %copy-start.3 = (f32[4,4096]{1,0:T(4,128)S(1)}, f32[4,4096]{1,0:T(4,128)}, u32[]{:S(2)}) copy-start(f32[4,4096]{1,0:T(4,128)} %param.11) | copy-start | bytes 196612
  331.6 7.3 %copy-start.4 = (s32[4096]{0:T(1024)S(1)}, s32[4096]{0:T(1024)}, u32[]{:S(2)}) copy-start(s32[4096]{0:T(1024)} %param.10) | copy-start | bytes 49156
  331.6 135.2 %all-to-all-start = ((f32[32,16,4,4,256]{4,0,3,2,1:T(8,128)}), f32[32,16,4,4,256]{4,0,3,2,1:T(8,128)}, u32[]{:S(2)}, u32[]{:S(2)}) async-start(f32[32,16,4,4,256]{4,0,3,2,1:T(8,128)} %select_multiply_fusion), calls=%async_computation | async-start | bytes 16777216 | tf_op jit(solution)/shard_map/all_to_all | solution.py:97
Sparse Core Ops, SparseCore 0:
  46.4 61.4 all-reduce.8
  113.7 59.4 all-reduce.14
  179.1 59.4 all-reduce.12
  244.5 59.5 all-reduce.10
where the time goes:
time: 527 us
  waiting for transfers between devices  372 us (71%)
  other arithmetic  91.8 us (17%)
  local copies, waits for them, and re-layouts  37.1 us (7%)
  between operations  13.3 us (3%)
  starting transfers between devices  12.3 us (2%)
    psum x3, waiting for transfers between devices, body(): total_all, weighted_all = lax.psum((weight_total, weighted), 'ang')  178 us
    all_to_all x1, waiting for transfers between devices, body(): lax.all_to_all(picked, 'det', split_axis=1, concat_axis=4, tiled=True)  128 us
    psum x1, waiting for transfers between devices, body(): gain_map = lax.psum(jnp.sum(detail, axis=0), 'ang') / angles  61.3 us
    reshape x1, other arithmetic, body(): return moved.reshape(ang_dev, MOST, RB, total_cols)  36.4 us
    reduce_sum x1, other arithmetic, body(): gain_map = lax.psum(jnp.sum(detail, axis=0), 'ang') / angles  19.3 us
    reduce_sum x3, other arithmetic, body(): weight_total = jnp.sum(weights, axis=0)  14.4 us
    reshape x1, local copies, waits for them, and re-layouts, body(): return moved.reshape(ang_dev, MOST, RB, total_cols)  12.2 us
  transfers between devices with their start and end apart: 7, of which 7 were waited for; matrix products, arithmetic and copies ran while one was open for 0% of the time, Pallas kernels for 0%

commit v1 on v0

--- a/solution.py
+++ b/solution.py
@@ -94,7 +94,10 @@
     corrected = projected - gain_map
     picked = slot_blocks(corrected, destinations, owners)
     relative_all = band_offsets - jnp.arange(total_cols, dtype=jnp.int32)
-    arrived = lax.all_to_all(picked, "det", split_axis=1, concat_axis=4, tiled=True)
+    arrived = jnp.concatenate(
+        lax.all_to_all(jnp.stack(jnp.split(picked, lax.axis_size("det"), axis=1)), "det", 0, 0),
+        axis=4,
+    )
     pad_widths = [(0, 0)] * (arrived.ndim - 1) + [(HB, HB)]
     widened_all = jnp.pad(arrived, pad_widths)
     moved = band_sum(widened_all, relative_all, band_weights, arrived.shape[-1])

time: 527 us -> 537 us (1.019)
  local copies, waits for them, and re-layouts: 37.1 us -> 50.4 us
    unnamed x14 -> x29, local copies, waits for them, and re-layouts: 7.55 us -> 20 us
where the time goes in v1:
time: 537 us; the launch traced here: 536 us
  waiting for transfers between devices  372 us (69%)
  other arithmetic  87.8 us (16%)
  local copies, waits for them, and re-layouts  50.4 us (9%)
  between operations  13.3 us (2%)
  starting transfers between devices  12.3 us (2%)
    psum x3, waiting for transfers between devices, body(): total_all, weighted_all = lax.psum((weight_total, weighted), 'ang')  178 us
    all_to_all x1, waiting for transfers between devices, body(): lax.all_to_all(jnp.stack(jnp.split(picked, lax.axis_size('det'), axis=1))...  128 us
    psum x1, waiting for transfers between devices, body(): gain_map = lax.psum(jnp.sum(detail, axis=0), 'ang') / angles  61.3 us
    reshape x1, other arithmetic, body(): return moved.reshape(ang_dev, MOST, RB, total_cols)  36.4 us
    unnamed x29, local copies, waits for them, and re-layouts  20 us
    reduce_sum x1, other arithmetic, body(): gain_map = lax.psum(jnp.sum(detail, axis=0), 'ang') / angles  19.3 us
    reduce_sum x3, other arithmetic, body(): weight_total = jnp.sum(weights, axis=0)  14.4 us
    reshape x1, local copies, waits for them, and re-layouts, body(): return moved.reshape(ang_dev, MOST, RB, total_cols)  12.2 us
  transfers between devices with their start and end apart: 7, of which 7 were waited for; matrix products, arithmetic and copies ran while one was open for 0% of the time, Pallas kernels for 0%

profile of v1, /device:TPU:6, one launch (start us, length us, event | category | flops | bytes accessed | tf_op | source)
XLA Modules:
  0.0 535.9 jit_solution(1971352100251218978)
XLA Ops:
  6.5 0.0 all-reduce.9.cloned.1.call-start
  6.5 5.5 %copy.34 = f32[32,128,256]{1,0,2:T(8,128)} copy(f32[32,128,256]{2,1,0:T(8,128)} %param.6) | data formatting | bytes 8388608 | tf_op args[0]
  12.0 0.1 copy.33
  12.1 0.0 copy-done.2
  12.2 0.1 copy.35
  12.2 3.0 log_negate_fusion
  15.3 2.0 copy-done
  17.3 3.5 collective-permute-start
  20.7 1.3 collective-permute-start.1
  22.0 0.0 copy-done.5
  22.1 0.5 collective-permute-done
  22.6 4.3 collective-permute-done.1
  26.9 19.3 %fusion.52 = (f32[128,256]{0,1:T(8,128)}, f32[32,128,256]{1,0,2:T(8,128)}) fusion(f32[32,128,256]{1,0,2:T(8,128)} %copy-done, f32[256]{0:T(256)S(1)} %add_convert_fusion, f32[32,128,4]{1,0,2:T(8,128)S(1)} %collective-permute-done.1, f32[32,128,4]{1,0,2:T(8,128)S(1)} %collective-permute-done), kind=kLoop, calls=%fused_computation.144 | loop fusion | flops 19890176 | bytes 8651776 | tf_op jit(solution)/shard_map/reduce_sum | solution.py:86
  46.2 0.0 all-reduce.9.cloned.1.call-update
  46.2 0.0 all-reduce.15.cloned.1.call-start
  46.3 0.2 convert_reduce_fusion
  46.4 61.3 %all-reduce.9.cloned.1.call-done = f32[128,256]{0,1:T(8,128)} async-done(((f32[128,256]{0,1:T(8,128)}), f32[128,256]{0,1:T(8,128)}) %all-reduce.9.cloned.1.call-update) | async-done | bytes 131088 | tf_op jit(solution)/shard_map/psum | solution.py:86
  107.8 0.9 broadcast_multiply_fusion
  108.7 4.8 fusion.29
  113.5 0.0 all-reduce.15.cloned.1.call-update
  113.5 0.0 all-reduce.13.cloned.1.call-start
  113.6 0.2 fusion.49
  113.8 0.1 copy.37
  113.9 0.1 reshape.187
  114.0 59.1 %all-reduce.15.cloned.1.call-done = (f32[128,256]{0,1:T(8,128)}, f32[128,256]{0,1:T(8,128)}) async-done(((f32[128,256]{0,1:T(8,128)}, f32[128,256]{0,1:T(8,128)}), (f32[128,256]{0,1:T(8,128)}, f32[128,256]{0,1:T(8,128)})) %all-reduce.15.cloned.1.call-update) | async-done | bytes 262160 | tf_op jit(solution)/shard_map/psum | solution.py:92
  173.1 1.0 div.57
  174.1 4.8 fusion.30
  178.9 0.0 all-reduce.13.cloned.1.call-update
  178.9 0.2 all-reduce.11.cloned.1.call-start
  179.2 59.4 %all-reduce.13.cloned.1.call-done = (f32[128,256]{0,1:T(8,128)}, f32[128,256]{0,1:T(8,128)}) async-done(((f32[128,256]{0,1:T(8,128)}, f32[128,256]{0,1:T(8,128)}), (f32[128,256]{0,1:T(8,128)}, f32[128,256]{0,1:T(8,128)})) %all-reduce.13.cloned.1.call-update) | async-done | bytes 262160 | tf_op jit(solution)/shard_map/psum | solution.py:92
  238.6 1.0 div.60
  239.6 4.8 fusion.31
  244.4 0.0 all-reduce.11.cloned.1.call-update
  244.4 0.1 copy.32
  244.5 0.1 copy.38
  244.6 59.5 %all-reduce.11.cloned.1.call-done = (f32[128,256]{0,1:T(8,128)}, f32[128,256]{0,1:T(8,128)}) async-done(((f32[128,256]{0,1:T(8,128)}, f32[128,256]{0,1:T(8,128)}), (f32[128,256]{0,1:T(8,128)}, f32[128,256]{0,1:T(8,128)})) %all-reduce.11.cloned.1.call-update) | async-done | bytes 262160 | tf_op jit(solution)/shard_map/psum | solution.py:92
  304.1 1.0 div.63
  305.1 5.4 %broadcast_subtract_fusion = f32[32,128,256]{1,0,2:T(8,128)} fusion(f32[128,256]{0,1:T(8,128)S(1)} %div.63, f32[128,256]{0,1:T(8,128)S(1)} %copy.35, f32[32,128,256]{1,0,2:T(8,128)} %copy.34, f32[128,256]{0,1:T(8,128)S(1)} %copy.33), kind=kLoop, calls=%fused_computation.59 | loop fusion | flops 4194304 | bytes 8781824 | tf_op jit(solution)/shard_map/sub | solution.py:94
  310.5 5.6 %copy.36 = f32[32,128,256]{2,0,1:T(8,128)} copy(f32[32,128,256]{1,0,2:T(8,128)} %broadcast_subtract_fusion) | data formatting | bytes 8388608 | tf_op jit(solution)/shard_map/sub | solution.py:94
  316.1 6.7 %gather_fusion = f32[64,32,4,256]{3,1,2,0:T(8,128)} fusion(f32[32,32,4,256]{3,0,2,1:T(8,128)} %bitcast.80, s32[1024]{0:T(1024)S(1)} %pad_clamp_fusion), kind=kCustom, calls=%fused_computation | custom fusion | bytes 16777472 | tf_op jit(solution)/shard_map/jit(_take)/gather | solution.py:72
  322.8 4.9 select_multiply_fusion
  327.7 0.8 fusion.47
  328.5 0.8 fusion.46
  329.3 0.8 fusion.45
  330.2 0.8 fusion.44
  331.0 0.8 fusion.43
  331.8 0.8 fusion.42
  332.7 0.8 fusion.41
  333.5 0.8 fusion.40
  334.3 0.8 fusion.39
  335.2 0.8 fusion.38
  336.0 0.8 fusion.37
  336.8 0.8 fusion.36
  337.6 0.8 fusion.35
  338.5 0.8 fusion.34
  339.3 0.8 fusion.33
  340.1 0.8 fusion.32
  341.0 7.2 %all-to-all-start = ((f32[16,32,1,4,4,256]{5,1,4,3,2,0:T(8,128)}), f32[16,32,1,4,4,256]{5,1,4,3,2,0:T(8,128)}, u32[]{:S(2)}, u32[]{:S(2)}) async-start(f32[16,32,1,4,4,256]{5,1,4,3,2,0:T(8,128)} %fusion.32), calls=%async_computation | async-start | bytes 16777216 | tf_op jit(solution)/shard_map/all_to_all | solution.py:98
  348.2 0.0 copy-done.4
  348.2 0.1 select_add_fusion.16
  348.3 127.9 %all-to-all-done = f32[16,32,1,4,4,256]{5,1,4,3,2,0:T(8,128)} async-done(((f32[16,32,1,4,4,256]{5,1,4,3,2,0:T(8,128)}), f32[16,32,1,4,4,256]{5,1,4,3,2,0:T(8,128)}, u32[]{:S(2)}, u32[]{:S(2)}) %all-to-all-start) | async-done | bytes 8388640 | tf_op jit(solution)/shard_map/all_to_all | solution.py:98
  476.2 4.6 copy.41
  480.8 36.4 %add_bitcast_fusion = f32[32,4,4,4096]{3,0,2,1:T(8,128)} fusion(f32[32,1,4,4,4096]{4,0,3,2,1:T(8,128)S(1)} %bitcast.81, f32[4096]{0:T(1024)S(1)} %get-tuple-element.24, f32[4096]{0:T(1024)S(1)} %get-tuple-element.25, f32[4096]{0:T(1024)S(1)} %get-tuple-element.26, f32[4096]{0:T(1024)S(1)} %get-tuple-element.27, f32[4096]{0:T(1024)S(1)} %get-tuple-element.28, ...), kind=kLoop, calls=%fused_computation.1 | loop fusion | flops 69206016 | bytes 17055744 | tf_op jit(solution)/shard_map/reshape | solution.py:104
  517.2 12.2 %copy.40 = f32[32,4,4,4096]{3,2,1,0:T(4,128)} copy(f32[32,4,4,4096]{3,0,2,1:T(8,128)} %add_bitcast_fusion) | data formatting | bytes 16777216 | tf_op jit(solution)/shard_map/reshape | solution.py:104
  (18 shorter events, 0.1 us)
Async XLA Ops:
  6.5 5.5 %copy-start.1 = (f32[128,256]{1,0:T(8,128)S(1)}, f32[128,256]{1,0:T(8,128)}, u32[]{:S(2)}) copy-start(f32[128,256]{1,0:T(8,128)} %param.7) | copy-start | bytes 393220
  6.5 5.6 %copy-start.2 = (f32[128,256]{1,0:T(8,128)S(1)}, f32[128,256]{1,0:T(8,128)}, u32[]{:S(2)}) copy-start(f32[128,256]{1,0:T(8,128)} %param.8) | copy-start | bytes 393220
  6.5 15.5 %copy-start.5 = (s32[32,1]{0,1:T(1,128)S(1)}, s32[32,1]{0,1:T(1,128)}, u32[]{:S(2)}) copy-start(s32[32,1]{0,1:T(1,128)} %param.9) | copy-start | bytes 388
  6.5 101.2 %all-reduce.9.cloned.1.call-start = ((), (), s32[]{:S(2)}) async-start(), calls=%async_computation.1 | async-start | bytes 262144 | tf_op jit(solution)/shard_map/psum | solution.py:86
  15.3 2.0 copy-start
  17.3 5.4 %collective-permute-start = (f32[32,128,4]{1,0,2:T(8,128)S(1)}, f32[32,128,4]{1,0,2:T(8,128)S(1)}, u32[]{:S(2)}, u32[]{:S(2)}) collective-permute-start(f32[32,128,4]{1,0,2:T(8,128)S(1)} %get-tuple-element.21), channel_id=1, source_target_pairs={{0,1},{1,2},{2,3},{3,4},{4,5},{5,6},{6,7},{7,8},{8,9},{9,10},{10,1... | collective-permute-start | bytes 196616 | tf_op jit(solution)/shard_map/ppermute | solution.py:22
  20.7 6.2 %collective-permute-start.1 = (f32[32,128,4]{1,0,2:T(8,128)S(1)}, f32[32,128,4]{1,0,2:T(8,128)S(1)}, u32[]{:S(2)}, u32[]{:S(2)}) collective-permute-start(f32[32,128,4]{1,0,2:T(8,128)S(1)} %get-tuple-element.22), channel_id=1, source_target_pairs={{1,0},{2,1},{3,2},{4,3},{5,4},{6,5},{7,6},{8,7},{9,8},{10,9},{11,1... | collective-permute-start | bytes 196616 | tf_op jit(solution)/shard_map/ppermute | solution.py:23
  46.2 126.9 %all-reduce.15.cloned.1.call-start = ((), (), s32[]{:S(2)}) async-start(), calls=%async_computation.4 | async-start | bytes 524288 | tf_op jit(solution)/shard_map/psum | solution.py:92
  113.5 125.0 %all-reduce.13.cloned.1.call-start = ((), (), s32[]{:S(2)}) async-start(), calls=%async_computation.3 | async-start | bytes 524288 | tf_op jit(solution)/shard_map/psum | solution.py:92
  178.9 125.1 %all-reduce.11.cloned.1.call-start = ((), (), s32[]{:S(2)}) async-start(), calls=%async_computation.2 | async-start | bytes 524288 | tf_op jit(solution)/shard_map/psum | solution.py:92
  341.0 7.2 %copy-start.3 = (f32[4,4096]{1,0:T(4,128)S(1)}, f32[4,4096]{1,0:T(4,128)}, u32[]{:S(2)}) copy-start(f32[4,4096]{1,0:T(4,128)} %param.11) | copy-start | bytes 196612
  341.0 7.3 %copy-start.4 = (s32[4096]{0:T(1024)S(1)}, s32[4096]{0:T(1024)}, u32[]{:S(2)}) copy-start(s32[4096]{0:T(1024)} %param.10) | copy-start | bytes 49156
  341.0 135.2 %all-to-all-start = ((f32[16,32,1,4,4,256]{5,1,4,3,2,0:T(8,128)}), f32[16,32,1,4,4,256]{5,1,4,3,2,0:T(8,128)}, u32[]{:S(2)}, u32[]{:S(2)}) async-start(f32[16,32,1,4,4,256]{5,1,4,3,2,0:T(8,128)} %fusion.32), calls=%async_computation | async-start | bytes 16777216 | tf_op jit(solution)/shard_map/all_to_all | solution.py:98
Sparse Core Ops, SparseCore 0:
  46.3 61.4 all-reduce.8
  113.7 59.4 all-reduce.14
  179.1 59.4 all-reduce.12
  244.5 59.5 all-reduce.10
